TPU v7x, 512 devices: a whole 4x4x16 slice. The times are simulated.
512 devices in a mesh: dp: 32 (over z, core), seq: 16 (over y, x).
Axes of the slice: x: 4, y: 4, z: 16, core: 2. Of those that a mesh axis runs over, the one named last changes fastest.
Arguments:
- features: bfloat16 [32, 3072, 1024], P('dp', 'seq'), may hold values from -18 to 18
- qkv_weight: bfloat16 [1024, 3072], P('dp'), may hold values from -1 to 1
- cotangent: bfloat16 [32, 3072, 1024], P('dp', 'seq'), may hold values from -6 to 6
- node_order: int32 [32, 3072], P('dp'), may hold values from 0 to 3071, as said below
- blocks: int32 [32, 48, 8], P('dp'), may hold values from 0 to 47, as said below
- counts: int32 [32, 48], P('dp'), may hold values from 1 to 8, as said below
Outputs:
- attended: bfloat16 [32, 3072, 1024], P('dp', 'seq')
- grad_features: bfloat16 [32, 3072, 1024], P('dp', 'seq')
- grad_weight: float32 [1024, 3072], P('dp', 'seq')
Inputs may be any that keep to these rules, and one draw needn't show every extreme that they name: Every row of node_order lists each node of the subgraph once. blocks[g, c, 0] is c, and the 8 entries of a row are distinct clusters; slots at or beyond counts[g, c] are unused. `counts`: every subgraph has a cluster with all 8 slots live.
All inputs are finite; a program needn't handle non-finite values.
Results may differ from a plain program's by a relative error of at most 0.03.
Values may be sent and summed in bfloat16 or wider, within the bound.
No kernel may reach another device: no remote copies, remote signals or barrier semaphores. Data moves between devices by JAX's collectives and lax.ppermute only.
A program may use at most 128 MiB of HBM per device.

v0:
```python
import math
import jax
import jax.numpy as jnp
from jax import lax
from jax.sharding import PartitionSpec as P

HEADS = 16
HD = 64


def attend(query, key_in, value, grad_out, blocks, counts):
    cluster_count, slot_count = blocks.shape
    node_count, head_width = query.shape
    block_rows = node_count // cluster_count
    in_group = math.gcd(cluster_count, 8)
    runs_total = cluster_count // in_group
    score_scale = 1.0 / math.sqrt(head_width)
    key_blocks = key_in.reshape(cluster_count, block_rows, head_width)
    value_blocks = value.reshape(cluster_count, block_rows, head_width)
    inputs_all = (
        query.reshape(runs_total, in_group, block_rows, head_width),
        grad_out.reshape(runs_total, in_group, block_rows, head_width),
        blocks.reshape(runs_total, in_group, slot_count),
        counts.reshape(runs_total, in_group),
    )

    def group_step(totals, inputs_now):
        grad_key, grad_value = totals
        query_block, grad_block, block_ids, live_count = inputs_now
        key_rows = key_blocks[block_ids].reshape(in_group, slot_count * block_rows, head_width)
        value_rows = value_blocks[block_ids].reshape(in_group, slot_count * block_rows, head_width)
        is_live = jnp.repeat(
            jnp.arange(slot_count)[None, :] < live_count[:, None], block_rows, axis=1
        )[:, None, :]
        scores = (
            jnp.einsum("cqe,cke->cqk", query_block, key_rows, preferred_element_type=jnp.float32)
            * score_scale
        )
        scores = jnp.where(is_live, scores, -1e30)
        row_max = jnp.max(scores, axis=-1, keepdims=True)
        raw_weights = jnp.where(is_live, jnp.exp(scores - row_max), 0.0)
        attn_weights = raw_weights / jnp.sum(raw_weights, axis=-1, keepdims=True)
        attn_low = attn_weights.astype(jnp.bfloat16)
        output_blk = jnp.einsum(
            "cqk,cke->cqe", attn_low, value_rows, preferred_element_type=jnp.float32
        ).astype(jnp.bfloat16)
        grad_weights = jnp.einsum(
            "cqe,cke->cqk", grad_block, value_rows, preferred_element_type=jnp.float32
        )
        row_dot = jnp.sum(attn_weights * grad_weights, axis=-1, keepdims=True)
        grad_scores = (attn_weights * (grad_weights - row_dot) * score_scale).astype(jnp.bfloat16)
        grad_query = jnp.einsum(
            "cqk,cke->cqe", grad_scores, key_rows, preferred_element_type=jnp.float32
        ).astype(jnp.bfloat16)
        key_terms = jnp.einsum(
            "cqk,cqe->cke", grad_scores, query_block, preferred_element_type=jnp.float32
        )
        value_terms = jnp.einsum(
            "cqk,cqe->cke", attn_low, grad_block, preferred_element_type=jnp.float32
        )
        grad_key = grad_key.at[block_ids].add(
            key_terms.reshape(in_group, slot_count, block_rows, head_width)
        )
        grad_value = grad_value.at[block_ids].add(
            value_terms.reshape(in_group, slot_count, block_rows, head_width)
        )
        return ((grad_key, grad_value), (output_blk, grad_query))

    empty_sum = jnp.zeros((cluster_count, block_rows, head_width), jnp.float32)
    (grad_key, grad_value), (output_all, grad_query) = lax.scan(
        group_step, (empty_sum, empty_sum), inputs_all
    )
    return (
        output_all.reshape(node_count, head_width),
        grad_query.reshape(node_count, head_width),
        grad_key.reshape(node_count, head_width).astype(jnp.bfloat16),
        grad_value.reshape(node_count, head_width).astype(jnp.bfloat16),
    )


def per_device(features, qkv_weight, cotangent, node_order, blocks, counts):
    local_rows = features.shape[1]
    model_width = features.shape[2]
    heads_local = HEADS // lax.axis_size("seq")
    three_width = 3 * HD
    node_feats = features[0]
    cot_heads = cotangent[0].reshape(local_rows, HEADS, HD)
    weights_all = lax.all_gather(qkv_weight, "dp", axis=0, tiled=True)
    node_all = lax.all_gather(node_feats, "seq", axis=0, tiled=True)
    node_count = node_all.shape[0]
    projected = jnp.dot(node_feats, weights_all, preferred_element_type=jnp.float32).astype(
        jnp.bfloat16
    )
    projected = projected.reshape(local_rows, HEADS, three_width)
    head_qkv, head_cot = (
        lax.all_to_all(projected, "seq", split_axis=1, concat_axis=0, tiled=True),
        lax.all_to_all(cot_heads, "seq", split_axis=1, concat_axis=0, tiled=True),
    )
    graph_order = node_order[0]
    inverse = (
        jnp.zeros((node_count,), jnp.int32)
        .at[graph_order]
        .set(jnp.arange(node_count, dtype=jnp.int32))
    )
    sorted_qkv = head_qkv[graph_order]
    sorted_cot = head_cot[graph_order]
    output_all, grad_query, grad_key, grad_value = jax.vmap(
        attend, in_axes=(1, 1, 1, 1, None, None), out_axes=1
    )(
        sorted_qkv[:, :, :HD],
        sorted_qkv[:, :, HD : 2 * HD],
        sorted_qkv[:, :, 2 * HD :],
        sorted_cot,
        blocks[0],
        counts[0],
    )
    grad_heads = jnp.concatenate([grad_query, grad_key, grad_value], axis=-1)[inverse]
    output_nodes = output_all[inverse]
    output_back, grad_back = (
        lax.all_to_all(output_nodes, "seq", split_axis=0, concat_axis=1, tiled=True),
        lax.all_to_all(grad_heads, "seq", split_axis=0, concat_axis=1, tiled=True),
    )
    attended = output_back.reshape(1, local_rows, model_width)
    grad_local = grad_back.reshape(local_rows, 3 * model_width)
    grad_feats = lax.dot_general(
        grad_local, weights_all, (((1,), (1,)), ((), ())), preferred_element_type=jnp.float32
    )
    grad_features = grad_feats.astype(jnp.bfloat16).reshape(1, local_rows, model_width)
    head_grads = grad_heads.reshape(node_count, heads_local * three_width)
    grad_weight = lax.psum_scatter(
        lax.dot_general(
            node_all, head_grads, (((0,), (0,)), ((), ())), preferred_element_type=jnp.float32
        ).astype(jnp.bfloat16),
        "dp",
        scatter_dimension=0,
        tiled=True,
    ).astype(jnp.float32)
    return (attended, grad_features, grad_weight)


def solution(mesh):
    return jax.shard_map(
        per_device,
        mesh=mesh,
        in_specs=(
            P("dp", "seq", None),
            P("dp", None),
            P("dp", "seq", None),
            P("dp", None),
            P("dp", None, None),
            P("dp", None),
        ),
        out_specs=(P("dp", "seq", None), P("dp", "seq", None), P("dp", "seq")),
        check_vma=False,
    )
```

profile of v0, /device:TPU:8, one launch (start us, length us, event | category | flops | bytes accessed | tf_op | source)
XLA Modules:
  0.0 628.1 jit_solution(6024842970168261089)
XLA Ops:
  9.9 9.2 %all-to-all-start.1 = ((bf16[192,16,64]{0,2,1:T(8,128)(2,1)}), bf16[192,16,64]{0,2,1:T(8,128)(2,1)S(1)}, u32[]{:S(2)}, u32[]{:S(2)}) async-start(bf16[192,16,64]{0,2,1:T(8,128)(2,1)} %bitcast.27), calls=%async_computation.1 | async-start | bytes 1048576 | tf_op jit(solution)/shard_map/all_to_all | solution.py:97
  21.2 70.2 %all-gather.4.cloned.1.call-done = bf16[1024,3072]{1,0:T(8,128)(2,1)} async-done(((bf16[32,3072]{1,0:T(8,128)(2,1)}), bf16[1024,3072]{1,0:T(8,128)(2,1)}) %all-gather.4.cloned.1.call-update) | async-done | bytes 6291472 | tf_op jit(solution)/shard_map/all_gather | solution.py:88
  91.5 5.3 convolution_convert_fusion.2
  101.5 7.4 %all-to-all-start = ((bf16[192,16,192]{2,0,1:T(8,128)(2,1)}), bf16[192,16,192]{2,0,1:T(8,128)(2,1)S(1)}, u32[]{:S(2)}, u32[]{:S(2)}) async-start(bf16[192,16,192]{2,0,1:T(8,128)(2,1)} %copy.93), calls=%async_computation | async-start | bytes 3145728 | tf_op jit(solution)/shard_map/all_to_all | solution.py:96
  108.9 12.0 %scatter_custom_fusion.2 = s32[3072]{0:T(1024)S(1)} fusion(s32[3072]{0:T(1024)S(1)} %bitcast.182, s32[3072]{0:T(1024)S(1)} %iota.7, s32[]{:T(128)} %copy.139), kind=kCustom, calls=%fused_computation.71 | custom fusion | bytes 12292 | tf_op jit(solution)/shard_map/scatter | solution.py:103
  121.3 11.4 %gather_fusion.3 = bf16[3072,64]{1,0:T(8,128)(2,1)} fusion(bf16[3072,64]{1,0:T(8,128)(2,1)S(1)} %bitcast.161, s32[3072]{0:T(1024)S(1)} %broadcast_clamp_fusion), kind=kCustom, calls=%fused_computation.3 | custom fusion | bytes 798720 | tf_op jit(solution)/shard_map/gather | solution.py:106
  132.7 4.4 all-to-all-done
  137.2 11.1 %gather_fusion.2 = bf16[3072,192]{1,0:T(8,128)(2,1)S(1)} fusion(bf16[3072,192]{1,0:T(8,128)(2,1)S(1)} %bitcast.152, s32[3072]{0:T(1024)S(1)} %broadcast_clamp_fusion), kind=kCustom, calls=%fused_computation.2 | custom fusion | bytes 2371584 | tf_op jit(solution)/shard_map/gather | solution.py:105
  150.4 286.3 %while.16 = (s32[]{:T(128)}, f32[1,48,64,64]{3,2,1,0:T(8,128)S(1)}, f32[1,48,64,64]{3,2,1,0:T(8,128)S(1)}, bf16[6,1,8,64,64]{4,3,2,1,0:T(8,128)(2,1)}, bf16[6,1,...) while((s32[]{:T(128)}, f32[1,48,64,64]{3,2,1,0:T(8,128)S(1)}, ...), condition=%wide.region_6.7_spmd, body=%wide.region_0.6_spmd.sunk | while | flops 209000192 | bytes 36499064 | solution.py:70
  163.3 6.0 fusion.113
  169.3 4.3 fusion.111
  173.6 7.0 %scatter_fusion.1 = f32[48,64,64]{2,1,0:T(8,128)S(1)} fusion(f32[48,64,64]{2,1,0:T(8,128)S(1)} %bitcast.155, s32[64]{0:T(128)S(1)} %reshape.343, f32[64,64,64]{2,1,0:T(8,128)} %bitcast.163), kind=kCustom, calls=%fused_computation.7.clone.1 | custom fusion | flops 262144 | bytes 3145984 | tf_op jit(solution)/shard_map/vmap()/while/body/eval_jaxpr/scatter-add | solution.py:64
  180.6 7.0 %fusion.110 = f32[8,512,64]{2,1,0:T(8,128)} fusion(f32[8,64,512]{2,1,0:T(8,128)} %fusion.106, bf16[6,1,8,64,64]{4,3,2,1,0:T(8,128)(2,1)} %get-tuple-element.266, s32[]{:T(128)} %get-tuple-element.247, f32[8,64,512]{2,1,0:T(8,128)} %get-tuple-element.233, f32[8,64]{1,0:T(8,128)S(1)} %get-tuple-element.234), kind=kOutput, calls=%fused_computation.26.clone.1 | convolution fusion | flops 35390464 | bytes 5382656 | tf_op jit(solution)/shard_map/vmap()/while/body/eval_jaxpr/reshape | solution.py:62
  187.7 7.0 %scatter_fusion = f32[48,64,64]{2,1,0:T(8,128)S(1)} fusion(f32[48,64,64]{2,1,0:T(8,128)S(1)} %bitcast.153, s32[64]{0:T(128)S(1)} %reshape.343, f32[64,64,64]{2,1,0:T(8,128)} %bitcast.162), kind=kCustom, calls=%fused_computation.6.clone.1 | custom fusion | flops 262144 | bytes 3145984 | tf_op jit(solution)/shard_map/vmap()/while/body/eval_jaxpr/scatter-add | solution.py:61
  211.0 6.0 fusion.113
  217.1 4.3 fusion.111
  221.3 7.0 %scatter_fusion.1 = f32[48,64,64]{2,1,0:T(8,128)S(1)} fusion(f32[48,64,64]{2,1,0:T(8,128)S(1)} %bitcast.155, s32[64]{0:T(128)S(1)} %reshape.343, f32[64,64,64]{2,1,0:T(8,128)} %bitcast.163), kind=kCustom, calls=%fused_computation.7.clone.1 | custom fusion | flops 262144 | bytes 3145984 | tf_op jit(solution)/shard_map/vmap()/while/body/eval_jaxpr/scatter-add | solution.py:64
  228.3 7.0 %fusion.110 = f32[8,512,64]{2,1,0:T(8,128)} fusion(f32[8,64,512]{2,1,0:T(8,128)} %fusion.106, bf16[6,1,8,64,64]{4,3,2,1,0:T(8,128)(2,1)} %get-tuple-element.266, s32[]{:T(128)} %get-tuple-element.247, f32[8,64,512]{2,1,0:T(8,128)} %get-tuple-element.233, f32[8,64]{1,0:T(8,128)S(1)} %get-tuple-element.234), kind=kOutput, calls=%fused_computation.26.clone.1 | convolution fusion | flops 35390464 | bytes 5382656 | tf_op jit(solution)/shard_map/vmap()/while/body/eval_jaxpr/reshape | solution.py:62
  235.4 7.0 %scatter_fusion = f32[48,64,64]{2,1,0:T(8,128)S(1)} fusion(f32[48,64,64]{2,1,0:T(8,128)S(1)} %bitcast.153, s32[64]{0:T(128)S(1)} %reshape.343, f32[64,64,64]{2,1,0:T(8,128)} %bitcast.162), kind=kCustom, calls=%fused_computation.6.clone.1 | custom fusion | flops 262144 | bytes 3145984 | tf_op jit(solution)/shard_map/vmap()/while/body/eval_jaxpr/scatter-add | solution.py:61
  258.8 6.0 fusion.113
  264.8 4.3 fusion.111
  269.0 7.0 %scatter_fusion.1 = f32[48,64,64]{2,1,0:T(8,128)S(1)} fusion(f32[48,64,64]{2,1,0:T(8,128)S(1)} %bitcast.155, s32[64]{0:T(128)S(1)} %reshape.343, f32[64,64,64]{2,1,0:T(8,128)} %bitcast.163), kind=kCustom, calls=%fused_computation.7.clone.1 | custom fusion | flops 262144 | bytes 3145984 | tf_op jit(solution)/shard_map/vmap()/while/body/eval_jaxpr/scatter-add | solution.py:64
  276.0 7.0 %fusion.110 = f32[8,512,64]{2,1,0:T(8,128)} fusion(f32[8,64,512]{2,1,0:T(8,128)} %fusion.106, bf16[6,1,8,64,64]{4,3,2,1,0:T(8,128)(2,1)} %get-tuple-element.266, s32[]{:T(128)} %get-tuple-element.247, f32[8,64,512]{2,1,0:T(8,128)} %get-tuple-element.233, f32[8,64]{1,0:T(8,128)S(1)} %get-tuple-element.234), kind=kOutput, calls=%fused_computation.26.clone.1 | convolution fusion | flops 35390464 | bytes 5382656 | tf_op jit(solution)/shard_map/vmap()/while/body/eval_jaxpr/reshape | solution.py:62
  283.1 7.0 %scatter_fusion = f32[48,64,64]{2,1,0:T(8,128)S(1)} fusion(f32[48,64,64]{2,1,0:T(8,128)S(1)} %bitcast.153, s32[64]{0:T(128)S(1)} %reshape.343, f32[64,64,64]{2,1,0:T(8,128)} %bitcast.162), kind=kCustom, calls=%fused_computation.6.clone.1 | custom fusion | flops 262144 | bytes 3145984 | tf_op jit(solution)/shard_map/vmap()/while/body/eval_jaxpr/scatter-add | solution.py:61
  306.5 6.0 fusion.113
  312.5 4.3 fusion.111
  316.7 7.0 %scatter_fusion.1 = f32[48,64,64]{2,1,0:T(8,128)S(1)} fusion(f32[48,64,64]{2,1,0:T(8,128)S(1)} %bitcast.155, s32[64]{0:T(128)S(1)} %reshape.343, f32[64,64,64]{2,1,0:T(8,128)} %bitcast.163), kind=kCustom, calls=%fused_computation.7.clone.1 | custom fusion | flops 262144 | bytes 3145984 | tf_op jit(solution)/shard_map/vmap()/while/body/eval_jaxpr/scatter-add | solution.py:64
  323.8 7.0 %fusion.110 = f32[8,512,64]{2,1,0:T(8,128)} fusion(f32[8,64,512]{2,1,0:T(8,128)} %fusion.106, bf16[6,1,8,64,64]{4,3,2,1,0:T(8,128)(2,1)} %get-tuple-element.266, s32[]{:T(128)} %get-tuple-element.247, f32[8,64,512]{2,1,0:T(8,128)} %get-tuple-element.233, f32[8,64]{1,0:T(8,128)S(1)} %get-tuple-element.234), kind=kOutput, calls=%fused_computation.26.clone.1 | convolution fusion | flops 35390464 | bytes 5382656 | tf_op jit(solution)/shard_map/vmap()/while/body/eval_jaxpr/reshape | solution.py:62
  330.8 7.0 %scatter_fusion = f32[48,64,64]{2,1,0:T(8,128)S(1)} fusion(f32[48,64,64]{2,1,0:T(8,128)S(1)} %bitcast.153, s32[64]{0:T(128)S(1)} %reshape.343, f32[64,64,64]{2,1,0:T(8,128)} %bitcast.162), kind=kCustom, calls=%fused_computation.6.clone.1 | custom fusion | flops 262144 | bytes 3145984 | tf_op jit(solution)/shard_map/vmap()/while/body/eval_jaxpr/scatter-add | solution.py:61
  354.2 6.0 fusion.113
  360.2 4.3 fusion.111
  364.4 7.0 %scatter_fusion.1 = f32[48,64,64]{2,1,0:T(8,128)S(1)} fusion(f32[48,64,64]{2,1,0:T(8,128)S(1)} %bitcast.155, s32[64]{0:T(128)S(1)} %reshape.343, f32[64,64,64]{2,1,0:T(8,128)} %bitcast.163), kind=kCustom, calls=%fused_computation.7.clone.1 | custom fusion | flops 262144 | bytes 3145984 | tf_op jit(solution)/shard_map/vmap()/while/body/eval_jaxpr/scatter-add | solution.py:64
  371.5 7.0 %fusion.110 = f32[8,512,64]{2,1,0:T(8,128)} fusion(f32[8,64,512]{2,1,0:T(8,128)} %fusion.106, bf16[6,1,8,64,64]{4,3,2,1,0:T(8,128)(2,1)} %get-tuple-element.266, s32[]{:T(128)} %get-tuple-element.247, f32[8,64,512]{2,1,0:T(8,128)} %get-tuple-element.233, f32[8,64]{1,0:T(8,128)S(1)} %get-tuple-element.234), kind=kOutput, calls=%fused_computation.26.clone.1 | convolution fusion | flops 35390464 | bytes 5382656 | tf_op jit(solution)/shard_map/vmap()/while/body/eval_jaxpr/reshape | solution.py:62
  378.5 7.0 %scatter_fusion = f32[48,64,64]{2,1,0:T(8,128)S(1)} fusion(f32[48,64,64]{2,1,0:T(8,128)S(1)} %bitcast.153, s32[64]{0:T(128)S(1)} %reshape.343, f32[64,64,64]{2,1,0:T(8,128)} %bitcast.162), kind=kCustom, calls=%fused_computation.6.clone.1 | custom fusion | flops 262144 | bytes 3145984 | tf_op jit(solution)/shard_map/vmap()/while/body/eval_jaxpr/scatter-add | solution.py:61
  401.9 6.0 fusion.113
  407.9 4.3 fusion.111
  412.2 7.0 %scatter_fusion.1 = f32[48,64,64]{2,1,0:T(8,128)S(1)} fusion(f32[48,64,64]{2,1,0:T(8,128)S(1)} %bitcast.155, s32[64]{0:T(128)S(1)} %reshape.343, f32[64,64,64]{2,1,0:T(8,128)} %bitcast.163), kind=kCustom, calls=%fused_computation.7.clone.1 | custom fusion | flops 262144 | bytes 3145984 | tf_op jit(solution)/shard_map/vmap()/while/body/eval_jaxpr/scatter-add | solution.py:64
  419.2 7.0 %fusion.110 = f32[8,512,64]{2,1,0:T(8,128)} fusion(f32[8,64,512]{2,1,0:T(8,128)} %fusion.106, bf16[6,1,8,64,64]{4,3,2,1,0:T(8,128)(2,1)} %get-tuple-element.266, s32[]{:T(128)} %get-tuple-element.247, f32[8,64,512]{2,1,0:T(8,128)} %get-tuple-element.233, f32[8,64]{1,0:T(8,128)S(1)} %get-tuple-element.234), kind=kOutput, calls=%fused_computation.26.clone.1 | convolution fusion | flops 35390464 | bytes 5382656 | tf_op jit(solution)/shard_map/vmap()/while/body/eval_jaxpr/reshape | solution.py:62
  426.2 7.0 %scatter_fusion = f32[48,64,64]{2,1,0:T(8,128)S(1)} fusion(f32[48,64,64]{2,1,0:T(8,128)S(1)} %bitcast.153, s32[64]{0:T(128)S(1)} %reshape.343, f32[64,64,64]{2,1,0:T(8,128)} %bitcast.162), kind=kCustom, calls=%fused_computation.6.clone.1 | custom fusion | flops 262144 | bytes 3145984 | tf_op jit(solution)/shard_map/vmap()/while/body/eval_jaxpr/scatter-add | solution.py:61
  438.9 9.2 %gather_fusion.4 = bf16[3072,64]{1,0:T(8,128)(2,1)S(1)} fusion(bf16[3072,64]{1,0:T(8,128)(2,1)S(1)} %bitcast.164, s32[3072]{0:T(1024)S(1)} %fusion.52), kind=kCustom, calls=%fused_computation.4 | custom fusion | bytes 798720 | tf_op jit(solution)/shard_map/gather | solution.py:118
  451.4 5.9 all-to-all-start.2
  459.1 11.1 %gather_fusion.5 = bf16[3072,192]{1,0:T(8,128)(2,1)S(1)} fusion(bf16[3072,192]{1,0:T(8,128)(2,1)S(1)} %maximum_bitcast_fusion, s32[3072]{0:T(1024)S(1)} %fusion.52), kind=kCustom, calls=%fused_computation.5 | custom fusion | bytes 2371584 | tf_op jit(solution)/shard_map/gather | solution.py:117
  474.5 7.3 %all-to-all-start.3 = ((bf16[16,2,18432]{2,1,0:T(2,128)(2,1)}), bf16[16,2,18432]{2,1,0:T(2,128)(2,1)}, u32[]{:S(2)}, u32[]{:S(2)}) async-start(bf16[16,2,18432]{2,1,0:T(2,128)(2,1)} %reshape.324), calls=%async_computation.3 | async-start | bytes 2359296 | tf_op jit(solution)/shard_map/all_to_all | solution.py:121
  481.8 4.2 fusion.48
  491.1 101.6 %reduce-scatter.4.cloned.1.call-done = bf16[32,192]{1,0:T(8,128)(2,1)} async-done(((bf16[1024,192]{1,0:T(8,128)(2,1)}), bf16[32,192]{1,0:T(8,128)(2,1)}) %reduce-scatter.4.cloned.1.call-update) | async-done | bytes 12304
  594.2 8.4 %reshape.325 = bf16[3072,1,192]{2,1,0:T(2,128)(2,1)S(1)} reshape(bf16[16,2,18432]{2,1,0:T(2,128)(2,1)} %all-to-all-done.3) | data formatting | bytes 2359296
  602.6 6.2 copy.102
  615.8 5.7 fusion.47
  (148 shorter events, 135.5 us)
Async XLA Ops:
  7.2 84.3 %copy-start.3 = (bf16[1,192,1024]{2,1,0:T(8,128)(2,1)S(1)}, bf16[1,192,1024]{2,1,0:T(8,128)(2,1)}, u32[]{:S(2)}) copy-start(bf16[1,192,1024]{2,1,0:T(8,128)(2,1)} %param.8) | copy-start | bytes 1179652
  7.2 12.7 %copy-start.5 = (s32[1,48,8]{1,2,0:T(8,128)S(1)}, s32[1,48,8]{1,2,0:T(8,128)}, u32[]{:S(2)}) copy-start(s32[1,48,8]{1,2,0:T(8,128)} %param.12) | copy-start | bytes 4612
  7.2 13.3 %copy-start.6 = (s32[1,48]{1,0:T(1,128)S(1)}, s32[1,48]{1,0:T(1,128)}, u32[]{:S(2)}) copy-start(s32[1,48]{1,0:T(1,128)} %param.13) | copy-start | bytes 580
  7.2 84.3 %all-gather.4.cloned.1.call-start = ((), (), s32[]{:S(2)}) async-start(), calls=%async_computation.5 | async-start | bytes 6488064 | tf_op jit(solution)/shard_map/all_gather | solution.py:88
  9.9 91.6 %all-to-all-start.1 = ((bf16[192,16,64]{0,2,1:T(8,128)(2,1)}), bf16[192,16,64]{0,2,1:T(8,128)(2,1)S(1)}, u32[]{:S(2)}, u32[]{:S(2)}) async-start(bf16[192,16,64]{0,2,1:T(8,128)(2,1)} %bitcast.27), calls=%async_computation.1 | async-start | bytes 1048576 | tf_op jit(solution)/shard_map/all_to_all | solution.py:97
  19.1 462.7 %all-gather.6.cloned.1.call-start = ((), (), s32[]{:S(2)}) async-start(), calls=%async_computation.6 | async-start | bytes 6684672 | tf_op jit(solution)/shard_map/all_gather | solution.py:89
  101.5 7.4 %copy-start.4 = (s32[1,3072]{1,0:T(1,128)S(1)}, s32[1,3072]{1,0:T(1,128)}, u32[]{:S(2)}) copy-start(s32[1,3072]{1,0:T(1,128)} %param.11) | copy-start | bytes 36868
  101.5 35.7 %all-to-all-start = ((bf16[192,16,192]{2,0,1:T(8,128)(2,1)}), bf16[192,16,192]{2,0,1:T(8,128)(2,1)S(1)}, u32[]{:S(2)}, u32[]{:S(2)}) async-start(bf16[192,16,192]{2,0,1:T(8,128)(2,1)} %copy.93), calls=%async_computation | async-start | bytes 3145728 | tf_op jit(solution)/shard_map/all_to_all | solution.py:96
  155.4 1.0 copy-start
  203.2 1.0 copy-start
  250.9 1.0 copy-start
  298.6 1.0 copy-start
  346.3 1.0 copy-start
  394.0 1.0 copy-start
  437.8 1.1 copy-start.1
  448.6 8.6 %copy-start.2 = (bf16[1,48,64,64]{3,2,1,0:T(8,128)(2,1)S(1)}, bf16[1,48,64,64]{3,2,1,0:T(8,128)(2,1)}, u32[]{:S(2)}) copy-start(bf16[1,48,64,64]{3,2,1,0:T(8,128)(2,1)} %convert_element_type.62) | copy-start | bytes 1179652
  451.4 23.1 %all-to-all-start.2 = ((bf16[16,2,6144]{2,1,0:T(2,128)(2,1)}), bf16[16,2,6144]{2,1,0:T(2,128)(2,1)S(1)}, u32[]{:S(2)}, u32[]{:S(2)}) async-start(bf16[16,2,6144]{2,1,0:T(2,128)(2,1)} %reshape.322), calls=%async_computation.2 | async-start | bytes 786432 | tf_op jit(solution)/shard_map/all_to_all | solution.py:120
  474.5 119.7 %all-to-all-start.3 = ((bf16[16,2,18432]{2,1,0:T(2,128)(2,1)}), bf16[16,2,18432]{2,1,0:T(2,128)(2,1)}, u32[]{:S(2)}, u32[]{:S(2)}) async-start(bf16[16,2,18432]{2,1,0:T(2,128)(2,1)} %reshape.324), calls=%async_computation.3 | async-start | bytes 2359296 | tf_op jit(solution)/shard_map/all_to_all | solution.py:121
  481.7 110.9 %reduce-scatter.4.cloned.1.call-start = ((), (), s32[]{:S(2)}) async-start(), calls=%async_computation.7 | async-start | bytes 540672
Sparse Core Ops, SparseCore 0:
  10.2 81.2 all-gather.3
  94.5 83.8 all-gather.5
  487.2 105.4 reduce-scatter.3
where the time goes:
time: 633 us; the launch traced here: 628 us
  waiting for transfers between devices  178 us (28%)
  matrix products  168 us (27%)
  local copies, waits for them, and re-layouts  140 us (22%)
  other arithmetic  99 us (16%)
  starting transfers between devices  29.8 us (5%)
  between operations  14 us (2%)
    unnamed x4, waiting for transfers between devices  103 us
    all_gather x1, waiting for transfers between devices, per_device(): weights_all = lax.all_gather(qkv_weight, 'dp', axis=0, tiled=True)  70.2 us
    reshape x6, matrix products, group_step(): key_terms.reshape(in_group, slot_count, block_rows, head_width)  42.2 us
    scatter-add x6, other arithmetic, group_step(): grad_value.at[block_ids]  42 us
    scatter-add x6, other arithmetic, group_step(): grad_key.at[block_ids]  42 us
    dot_general x6, matrix products, group_step(): jnp.einsum('cqk,cke->cqe', grad_scores, key_rows, preferred_element_type=...  36 us
    reshape x6, matrix products, group_step(): value_terms.reshape(in_group, slot_count, block_rows, head_width)  25.7 us
    dot_general x6, matrix products, group_step(): jnp.einsum('cqk,cke->cqe', attn_low, value_rows, preferred_element_type=j...  21 us
  transfers between devices with their start and end apart: 7, of which 3 were waited for; matrix products, arithmetic and copies ran while one was open for 59% of the time, Pallas kernels for 0%

commit v1 on v0

--- a/solution.py
+++ b/solution.py
@@ -85,7 +85,9 @@
     three_width = 3 * HD
     node_feats = features[0]
     cot_heads = cotangent[0].reshape(local_rows, HEADS, HD)
-    weights_all = lax.all_gather(qkv_weight, "dp", axis=0, tiled=True)
+    weights_all = jnp.concatenate(
+        lax.all_to_all(jnp.stack(lax.axis_size("dp") * [qkv_weight], axis=0), "dp", 0, 0), axis=0
+    )
     node_all = lax.all_gather(node_feats, "seq", axis=0, tiled=True)
     node_count = node_all.shape[0]
     projected = jnp.dot(node_feats, weights_all, preferred_element_type=jnp.float32).astype(

time: 633 us -> 847 us (1.34)
  the two profiles are of different devices: /device:TPU:8 before, /device:TPU:2 now
where the time goes in v1:
time: 847 us; the launch traced here: 843 us
  waiting for transfers between devices  374 us (44%)
  matrix products  168 us (20%)
  local copies, waits for them, and re-layouts  143 us (17%)
  other arithmetic  99 us (12%)
  starting transfers between devices  44.7 us (5%)
  between operations  14.3 us (2%)
    all_to_all x1, waiting for transfers between devices, per_device(): lax.all_to_all(jnp.stack(lax.axis_size('dp') * [qkv_weight], axis=0), 'dp...  272 us
    unnamed x3, waiting for transfers between devices  101 us
    reshape x6, matrix products, group_step(): key_terms.reshape(in_group, slot_count, block_rows, head_width)  42.2 us
    scatter-add x6, other arithmetic, group_step(): grad_value.at[block_ids]  42 us
    scatter-add x6, other arithmetic, group_step(): grad_key.at[block_ids]  42 us
    dot_general x6, matrix products, group_step(): jnp.einsum('cqk,cke->cqe', grad_scores, key_rows, preferred_element_type=...  36 us
    reshape x6, matrix products, group_step(): value_terms.reshape(in_group, slot_count, block_rows, head_width)  25.7 us
    dot_general x6, matrix products, group_step(): jnp.einsum('cqk,cke->cqe', attn_low, value_rows, preferred_element_type=j...  21 us
  transfers between devices with their start and end apart: 7, of which 3 were waited for; matrix products, arithmetic and copies ran while one was open for 44% of the time, Pallas kernels for 0%

profile of v1, /device:TPU:2, one launch (start us, length us, event | category | flops | bytes accessed | tf_op | source)
XLA Modules:
  0.0 842.5 jit_solution(5541352876828276165)
XLA Ops:
  7.2 4.3 stack.2
  11.5 15.7 %all-to-all-start = ((bf16[32,32,3072]{2,1,0:T(8,128)(2,1)}), bf16[32,32,3072]{2,1,0:T(8,128)(2,1)}, u32[]{:S(2)}, u32[]{:S(2)}) async-start(bf16[32,32,3072]{2,1,0:T(8,128)(2,1)} %stack.2), calls=%async_computation | async-start | bytes 12582912 | tf_op jit(solution)/shard_map/all_to_all | solution.py:89
  30.3 271.8 %all-to-all-done = bf16[32,32,3072]{2,1,0:T(8,128)(2,1)} async-done(((bf16[32,32,3072]{2,1,0:T(8,128)(2,1)}), bf16[32,32,3072]{2,1,0:T(8,128)(2,1)}, u32[]{:S(2)}, u32[]{:S(2)}) %all-to-all-start) | async-done | bytes 6291488 | tf_op jit(solution)/shard_map/all_to_all | solution.py:89
  302.2 7.5 all-to-all-start.2
  309.7 5.3 convolution_convert_fusion.2
  320.0 7.0 all-to-all-start.1
  327.1 12.0 %scatter_custom_fusion.2 = s32[3072]{0:T(1024)S(1)} fusion(s32[3072]{0:T(1024)S(1)} %bitcast.183, s32[3072]{0:T(1024)S(1)} %iota.7, s32[]{:T(128)} %copy.139), kind=kCustom, calls=%fused_computation.71 | custom fusion | bytes 12292 | tf_op jit(solution)/shard_map/scatter | solution.py:105
  339.5 11.4 %gather_fusion.3 = bf16[3072,64]{1,0:T(8,128)(2,1)} fusion(bf16[3072,64]{1,0:T(8,128)(2,1)S(1)} %bitcast.162, s32[3072]{0:T(1024)S(1)} %broadcast_clamp_fusion), kind=kCustom, calls=%fused_computation.3 | custom fusion | bytes 798720 | tf_op jit(solution)/shard_map/gather | solution.py:108
  350.9 11.1 %gather_fusion.2 = bf16[3072,192]{1,0:T(8,128)(2,1)S(1)} fusion(bf16[3072,192]{1,0:T(8,128)(2,1)S(1)} %bitcast.153, s32[3072]{0:T(1024)S(1)} %broadcast_clamp_fusion), kind=kCustom, calls=%fused_computation.2 | custom fusion | bytes 2371584 | tf_op jit(solution)/shard_map/gather | solution.py:107
  364.1 286.3 %while.16 = (s32[]{:T(128)}, f32[1,48,64,64]{3,2,1,0:T(8,128)S(1)}, f32[1,48,64,64]{3,2,1,0:T(8,128)S(1)}, bf16[6,1,8,64,64]{4,3,2,1,0:T(8,128)(2,1)}, bf16[6,1,...) while((s32[]{:T(128)}, f32[1,48,64,64]{3,2,1,0:T(8,128)S(1)}, ...), condition=%wide.region_6.7_spmd, body=%wide.region_0.6_spmd.sunk | while | flops 209000192 | bytes 36499064 | solution.py:70
  377.0 6.0 fusion.113
  383.0 4.3 fusion.111
  387.3 7.0 scatter_fusion.1
  394.3 7.0 fusion.110
  401.3 7.0 scatter_fusion
  424.7 6.0 fusion.113
  430.7 4.3 fusion.111
  435.0 7.0 scatter_fusion.1
  442.0 7.0 fusion.110
  449.0 7.0 scatter_fusion
  472.4 6.0 fusion.113
  478.4 4.3 fusion.111
  482.7 7.0 scatter_fusion.1
  489.7 7.0 fusion.110
  496.8 7.0 scatter_fusion
  520.2 6.0 fusion.113
  526.2 4.3 fusion.111
  530.4 7.0 scatter_fusion.1
  537.4 7.0 fusion.110
  544.5 7.0 scatter_fusion
  567.9 6.0 fusion.113
  573.9 4.3 fusion.111
  578.1 7.0 scatter_fusion.1
  585.2 7.0 fusion.110
  592.2 7.0 scatter_fusion
  615.6 6.0 fusion.113
  621.6 4.3 fusion.111
  625.9 7.0 scatter_fusion.1
  632.9 7.0 fusion.110
  639.9 7.0 scatter_fusion
  652.6 9.2 %gather_fusion.4 = bf16[3072,64]{1,0:T(8,128)(2,1)S(1)} fusion(bf16[3072,64]{1,0:T(8,128)(2,1)S(1)} %bitcast.165, s32[3072]{0:T(1024)S(1)} %fusion.52), kind=kCustom, calls=%fused_computation.4 | custom fusion | bytes 798720 | tf_op jit(solution)/shard_map/gather | solution.py:120
  665.1 7.2 all-to-all-start.3
  674.2 11.1 %gather_fusion.5 = bf16[3072,192]{1,0:T(8,128)(2,1)S(1)} fusion(bf16[3072,192]{1,0:T(8,128)(2,1)S(1)} %maximum_bitcast_fusion, s32[3072]{0:T(1024)S(1)} %fusion.52), kind=kCustom, calls=%fused_computation.5 | custom fusion | bytes 2371584 | tf_op jit(solution)/shard_map/gather | solution.py:119
  689.5 7.2 all-to-all-start.4
  706.1 100.7 %reduce-scatter.4.cloned.1.call-done = bf16[32,192]{1,0:T(8,128)(2,1)} async-done(((bf16[1024,192]{1,0:T(8,128)(2,1)}), bf16[32,192]{1,0:T(8,128)(2,1)}) %reduce-scatter.4.cloned.1.call-update) | async-done | bytes 12304
  808.4 8.4 reshape.331
  816.7 6.2 copy.102
  829.9 5.7 fusion.47
  (150 shorter events, 138.3 us)
Async XLA Ops:
  11.5 16.5 %copy-start.3 = (bf16[1,192,1024]{2,1,0:T(8,128)(2,1)S(1)}, bf16[1,192,1024]{2,1,0:T(8,128)(2,1)}, u32[]{:S(2)}) copy-start(bf16[1,192,1024]{2,1,0:T(8,128)(2,1)} %param.10) | copy-start | bytes 1179652
  11.5 17.5 %copy-start.6 = (s32[1,48,8]{1,2,0:T(8,128)S(1)}, s32[1,48,8]{1,2,0:T(8,128)}, u32[]{:S(2)}) copy-start(s32[1,48,8]{1,2,0:T(8,128)} %param.12) | copy-start | bytes 4612
  11.5 18.1 %copy-start.7 = (s32[1,48]{1,0:T(1,128)S(1)}, s32[1,48]{1,0:T(1,128)}, u32[]{:S(2)}) copy-start(s32[1,48]{1,0:T(1,128)} %param.13) | copy-start | bytes 580
  11.5 290.7 %all-to-all-start = ((bf16[32,32,3072]{2,1,0:T(8,128)(2,1)}), bf16[32,32,3072]{2,1,0:T(8,128)(2,1)}, u32[]{:S(2)}, u32[]{:S(2)}) async-start(bf16[32,32,3072]{2,1,0:T(8,128)(2,1)} %stack.2), calls=%async_computation | async-start | bytes 12582912 | tf_op jit(solution)/shard_map/all_to_all | solution.py:89
  27.2 282.4 %copy-start.4 = (bf16[1,192,1024]{2,1,0:T(8,128)(2,1)S(1)}, bf16[1,192,1024]{2,1,0:T(8,128)(2,1)}, u32[]{:S(2)}) copy-start(bf16[1,192,1024]{2,1,0:T(8,128)(2,1)} %param.8) | copy-start | bytes 1179652
  27.2 669.6 %all-gather.3.cloned.1.call-start = ((), (), s32[]{:S(2)}) async-start(), calls=%async_computation.6 | async-start | bytes 6684672 | tf_op jit(solution)/shard_map/all_gather | solution.py:91
  302.2 17.8 %all-to-all-start.2 = ((bf16[192,16,64]{0,2,1:T(8,128)(2,1)}), bf16[192,16,64]{0,2,1:T(8,128)(2,1)S(1)}, u32[]{:S(2)}, u32[]{:S(2)}) async-start(bf16[192,16,64]{0,2,1:T(8,128)(2,1)} %bitcast.28), calls=%async_computation.2 | async-start | bytes 1048576 | tf_op jit(solution)/shard_map/all_to_all | solution.py:99
  319.7 7.4 copy-start.5
  320.0 30.9 %all-to-all-start.1 = ((bf16[192,16,192]{2,0,1:T(8,128)(2,1)}), bf16[192,16,192]{2,0,1:T(8,128)(2,1)S(1)}, u32[]{:S(2)}, u32[]{:S(2)}) async-start(bf16[192,16,192]{2,0,1:T(8,128)(2,1)} %copy.93), calls=%async_computation.1 | async-start | bytes 3145728 | tf_op jit(solution)/shard_map/all_to_all | solution.py:98
  369.1 1.0 copy-start
  416.9 1.0 copy-start
  464.6 1.0 copy-start
  512.3 1.0 copy-start
  560.0 1.0 copy-start
  607.7 1.0 copy-start
  651.5 1.1 copy-start.1
  662.3 10.0 %copy-start.2 = (bf16[1,48,64,64]{3,2,1,0:T(8,128)(2,1)S(1)}, bf16[1,48,64,64]{3,2,1,0:T(8,128)(2,1)}, u32[]{:S(2)}) copy-start(bf16[1,48,64,64]{3,2,1,0:T(8,128)(2,1)} %convert_element_type.62) | copy-start | bytes 1179652
  665.1 24.5 %all-to-all-start.3 = ((bf16[16,2,6144]{2,1,0:T(2,128)(2,1)}), bf16[16,2,6144]{2,1,0:T(2,128)(2,1)S(1)}, u32[]{:S(2)}, u32[]{:S(2)}) async-start(bf16[16,2,6144]{2,1,0:T(2,128)(2,1)} %reshape.328), calls=%async_computation.3 | async-start | bytes 786432 | tf_op jit(solution)/shard_map/all_to_all | solution.py:122
  689.5 118.8 %all-to-all-start.4 = ((bf16[16,2,18432]{2,1,0:T(2,128)(2,1)}), bf16[16,2,18432]{2,1,0:T(2,128)(2,1)}, u32[]{:S(2)}, u32[]{:S(2)}) async-start(bf16[16,2,18432]{2,1,0:T(2,128)(2,1)} %reshape.330), calls=%async_computation.4 | async-start | bytes 2359296 | tf_op jit(solution)/shard_map/all_to_all | solution.py:123
  696.8 110.1 %reduce-scatter.4.cloned.1.call-start = ((), (), s32[]{:S(2)}) async-start(), calls=%async_computation.7 | async-start | bytes 540672
Sparse Core Ops, SparseCore 0:
  31.1 77.5 all-gather.2
  702.2 104.5 reduce-scatter.3
